TPU v7x, 128 devices: a whole 4x4x4 slice. The times are simulated.
128 devices in a mesh: dp: 2 (over core), context: 2 (over y_lo), expert: 32 (over z, x, y_hi).
Axes of the slice: x: 4, y: 4 (y_hi: 2, y_lo: 2; y = y_hi * 2 + y_lo), z: 4, core: 2. Of those that a mesh axis runs over, the one named last changes fastest.
Arguments:
- tokens: bfloat16 [64, 256, 2048], P(('dp', 'expert'), 'context'), may hold values from -16 to 16
- grad_output: bfloat16 [64, 256, 2048], P(('dp', 'expert'), 'context'), may hold values from -6 to 6
- routes: int32 [64, 256, 8], P(('dp', 'expert'), 'context'), may hold values from 0 to 31, all different within a row; in each aligned block of 128 rows (0 to 127, 128 to 255, ..., all dimensions but the last counted through in order) at most 40 rows name the same one
- positions: int32 [64, 256], P(('dp', 'expert')), may hold values from 0 to 255, as said below
- attn_gain: float32 [2048], replicated, may hold values from 0.5 to 1.5
- q_gain: float32 [2048], replicated, may hold values from 0.1 to 1.9
- k_gain: float32 [2048], replicated, may hold values from 0.1 to 1.9
- ffn_gain: float32 [2048], replicated, may hold values from 0.5 to 1.5
- qkv_weight: bfloat16 [3, 2048, 2048], P(None, ('dp', 'context', 'expert')), may hold values from -0.125 to 0.125
- out_weight: bfloat16 [2048, 2048], P(('dp', 'context', 'expert')), may hold values from -1 to 1
- router_weight: bfloat16 [2048, 32], replicated, may hold values from -0.25 to 0.25
- expert_in: bfloat16 [32, 2, 2048, 1024], P('expert'), may hold values from -0.125 to 0.125
- expert_out: bfloat16 [32, 1024, 2048], P('expert'), may hold values from -0.75 to 0.75
Outputs:
- output: float32 [64, 256, 2048], P(('dp', 'expert'), 'context')
- grad_tokens: float32 [64, 256, 2048], P(('dp', 'expert'), 'context')
- grad_attn_gain: float32 [2048], replicated
- grad_q_gain: float32 [2048], replicated
- grad_k_gain: float32 [2048], replicated
- grad_ffn_gain: float32 [2048], replicated
- grad_router: float32 [2048, 32], replicated
- grad_qkv_weight: float32 [3, 2048, 2048], P(None, ('dp', 'context', 'expert'))
- grad_out_weight: float32 [2048, 2048], P(('dp', 'context', 'expert'))
- grad_expert_in: float32 [32, 2, 2048, 1024], P('expert', None, ('dp', 'context'))
- grad_expert_out: float32 [32, 1024, 2048], P('expert', None, ('dp', 'context'))
Inputs may be any that keep to these rules, and one draw needn't show every extreme that they name: `routes`: each row names 8 different experts; the rows of one device name one expert at most 40 times. Each row is a permutation of the positions of one sequence.
All inputs are finite; a program needn't handle non-finite values.
Results may differ from a plain program's by a relative error of at most 0.019.
Values may be sent and summed in bfloat16 or wider, within the bound.
No kernel may reach another device: no remote copies, remote signals or barrier semaphores. Data moves between devices by JAX's collectives and lax.ppermute only.
A program may use at most 448 MiB of HBM per device.

v0:
```python
import jax
import jax.numpy as jnp
from jax import lax
from jax.sharding import PartitionSpec as P

HDIM = 128
EPS = 1e-05
THETA = 10000.0


def rope_tables(places, head_dim):
    half = head_dim // 2
    freq = THETA ** (-jnp.arange(half, dtype=jnp.float32) * 2.0 / head_dim)
    angle = places.astype(jnp.float32)[:, None] * freq[None, :]
    return (jnp.cos(angle), jnp.sin(angle))


def rotate(values, cosine, sine, sign):
    half = values.shape[-1] // 2
    first = values[..., :half]
    second = values[..., half:]
    cosine = cosine[:, None, :]
    sine = sign * sine[:, None, :]
    return jnp.concatenate(
        [first * cosine - second * sine, second * cosine + first * sine], axis=-1
    )


def rms_forward(values):
    factor = lax.rsqrt(jnp.mean(values * values, axis=-1, keepdims=True) + EPS)
    return (values * factor, factor)


def rms_backward(grad_out, normed, factor, gain):
    scaled = grad_out * gain
    grad_in = factor * (scaled - normed * jnp.mean(scaled * normed, axis=-1, keepdims=True))
    return (grad_in, jnp.sum(grad_out * normed, axis=0))


def slot_index(route_rows, experts, capacity):
    onehot = (route_rows[:, None] == jnp.arange(experts, dtype=jnp.int32)[None, :]).astype(
        jnp.int32
    )
    count = route_rows.shape[0]
    earlier = (
        jnp.arange(count, dtype=jnp.int32)[None, :] < jnp.arange(count, dtype=jnp.int32)[:, None]
    ).astype(jnp.bfloat16)
    before = jnp.dot(earlier, onehot.astype(jnp.bfloat16), preferred_element_type=jnp.float32)
    return route_rows * capacity + jnp.sum(before.astype(jnp.int32) * onehot, axis=1)


def expert_major(received, local_experts, capacity):
    sources, _, width = received.shape
    return (
        received.reshape(sources, local_experts, capacity, width)
        .transpose(1, 0, 2, 3)
        .reshape(local_experts, sources * capacity, width)
    )


def source_major(results, sources, capacity):
    local_experts, _, width = results.shape
    return (
        results.reshape(local_experts, sources, capacity, width)
        .transpose(1, 0, 2, 3)
        .reshape(sources, local_experts * capacity, width)
    )


def swap_context(values):
    return lax.ppermute(values, "context", [(0, 1), (1, 0)])


def gather_context(values):
    other = swap_context(values)
    first = lax.axis_index("context") == 0
    return jnp.concatenate(
        [jnp.where(first, values, other), jnp.where(first, other, values)], axis=0
    )


def sum_context_halves(values):
    half = values.shape[0] // 2
    first = lax.axis_index("context") == 0
    own = jnp.where(first, values[:half], values[half:])
    given = jnp.where(first, values[half:], values[:half]).astype(jnp.bfloat16)
    return own + swap_context(given).astype(own.dtype)


def butterfly_sum(values, axes):
    index = lax.axis_index(axes)
    count = 1
    for name in axes:
        count *= lax.axis_size(name)
    step = 1
    while step < count:
        partner = [(i, i ^ step) for i in range(count)]
        received = lax.ppermute(values, axes, partner)
        mine_first = index & step == 0
        values = jnp.where(mine_first, values + received, received + values)
        step *= 2
    return values


def body(
    tokens,
    grad_output,
    routes,
    positions,
    attn_gain,
    q_gain,
    k_gain,
    ffn_gain,
    qkv_weight,
    out_weight,
    router_weight,
    expert_in,
    expert_out,
):
    single_precision = jnp.float32
    bf16 = jnp.bfloat16
    seq_tok = tokens.shape[1]
    width = tokens.shape[2]
    top = routes.shape[2]
    heads_width = out_weight.shape[1]
    head_dim = HDIM
    heads = heads_width // head_dim
    local_experts = expert_in.shape[0]
    experts = router_weight.shape[1]
    sources = lax.axis_size("expert")
    capacity = min(seq_tok, seq_tok * top * 5 // (4 * experts))
    scale = head_dim ** (-0.5)
    x = tokens[0].astype(single_precision)
    normed1, factor1 = rms_forward(x)
    attention_input = (normed1 * attn_gain).astype(bf16)
    all_axes = ("dp", "context", "expert")
    weights_full = lax.all_gather(
        jnp.concatenate([qkv_weight.transpose(1, 0, 2), out_weight[:, None, :]], axis=1),
        all_axes,
        axis=0,
        tiled=True,
    )
    out_full = weights_full[:, 3, :]
    projected_all = jnp.dot(
        attention_input,
        weights_full.reshape(width, 4 * heads_width),
        preferred_element_type=single_precision,
    ).reshape(seq_tok, 4, heads_width)
    projected_output = projected_all[:, :3].transpose(1, 0, 2)
    q_normed, q_factor = rms_forward(projected_output[0])
    k_normed, k_factor = rms_forward(projected_output[1])
    values = projected_output[2].astype(bf16)
    all_places = positions[0]
    own_places = lax.dynamic_slice_in_dim(all_places, lax.axis_index("context") * seq_tok, seq_tok)
    cosine, sine = rope_tables(own_places, head_dim)
    queries = rotate(
        (q_normed * q_gain).reshape(seq_tok, heads, head_dim), cosine, sine, 1.0
    ).astype(bf16)
    own_keys = rotate(
        (k_normed * k_gain).reshape(seq_tok, heads, head_dim), cosine, sine, 1.0
    ).astype(bf16)
    keys_vals = gather_context(jnp.stack([own_keys.reshape(seq_tok, heads_width), values], axis=1))
    keys = keys_vals[:, 0]
    vals = keys_vals[:, 1]
    seq_len = keys.shape[0]
    keys3 = keys.reshape(seq_len, heads, head_dim)
    vals3 = vals.reshape(seq_len, heads, head_dim)
    allowed = (all_places[None, :] <= own_places[:, None])[None]

    def masked_scores():
        scores = (
            jnp.einsum("qhd,khd->hqk", queries, keys3, preferred_element_type=single_precision)
            * scale
        )
        return jnp.where(allowed, scores, -jnp.inf)

    scores = masked_scores()
    lse = jnp.log(jnp.sum(jnp.exp(scores), axis=-1, keepdims=True))
    probs_b = jnp.exp(scores - lse).astype(bf16)
    attended = (
        jnp.einsum("hqk,khd->qhd", probs_b, vals3, preferred_element_type=single_precision)
        .astype(bf16)
        .reshape(seq_tok, heads_width)
    )
    mid = x + jnp.einsum("tq,dq->td", attended, out_full, preferred_element_type=single_precision)
    normed2, factor2 = rms_forward(mid)
    ffn_in = (normed2 * ffn_gain).astype(bf16)
    router_exp = jnp.exp(jnp.dot(ffn_in, router_weight, preferred_element_type=single_precision))
    router_probs = router_exp / jnp.sum(router_exp, axis=-1, keepdims=True)
    own_routes = routes[0]
    slots = slot_index(own_routes.reshape(-1), experts, capacity)
    send = (
        jnp.zeros((experts * capacity, width), bf16).at[slots].set(jnp.repeat(ffn_in, top, axis=0))
    )
    received = lax.all_to_all(
        send.reshape(sources, local_experts * capacity, width),
        "expert",
        split_axis=0,
        concat_axis=0,
        tiled=True,
    )
    rows = expert_major(received, local_experts, capacity)
    gate_up = jnp.einsum("lrd,lkdh->lkrh", rows, expert_in, preferred_element_type=single_precision)
    gate = gate_up[:, 0]
    up = gate_up[:, 1]
    sig = jax.nn.sigmoid(gate)
    hidden = (gate * sig * up).astype(bf16)
    results = jnp.einsum(
        "lrh,lhd->lrd", hidden, expert_out, preferred_element_type=single_precision
    ).astype(bf16)
    back = lax.all_to_all(
        source_major(results, sources, capacity), "expert", split_axis=0, concat_axis=0, tiled=True
    )
    route_out = back.reshape(experts * capacity, width)[slots].reshape(seq_tok, top, width)
    route_weight = jnp.take_along_axis(router_probs, own_routes, axis=1)
    output = mid + jnp.sum(route_weight[:, :, None] * route_out, axis=1)
    grad = grad_output[0].astype(single_precision)
    route_grad_weight = jnp.sum(grad[:, None, :] * route_out, axis=-1)
    route_grad = (
        (route_weight[:, :, None] * grad[:, None, :]).astype(bf16).reshape(seq_tok * top, width)
    )
    grad_send = jnp.zeros((experts * capacity, width), bf16).at[slots].set(route_grad)
    grad_received = lax.all_to_all(
        grad_send.reshape(sources, local_experts * capacity, width),
        "expert",
        split_axis=0,
        concat_axis=0,
        tiled=True,
    )
    grad_rows = expert_major(grad_received, local_experts, capacity)
    grad_hidden = jnp.einsum(
        "lrd,lhd->lrh", grad_rows, expert_out, preferred_element_type=single_precision
    )
    grad_down = jnp.einsum(
        "lrh,lrd->lhd", hidden, grad_rows, preferred_element_type=single_precision
    )
    grad_gate = (grad_hidden * up * sig * (1.0 + gate * (1.0 - sig))).astype(bf16)
    grad_up = (grad_hidden * gate * sig).astype(bf16)
    grad_gate_up = jnp.stack([grad_gate, grad_up], axis=1)
    grad_gate_up_w = jnp.einsum(
        "lrd,lkrh->lkdh", rows, grad_gate_up, preferred_element_type=single_precision
    )
    grad_rows_in = jnp.einsum(
        "lkrh,lkdh->lrd", grad_gate_up, expert_in, preferred_element_type=single_precision
    ).astype(bf16)
    grad_back = lax.all_to_all(
        source_major(grad_rows_in, sources, capacity),
        "expert",
        split_axis=0,
        concat_axis=0,
        tiled=True,
    )
    grad_route_in = grad_back.reshape(experts * capacity, width)[slots].reshape(seq_tok, top, width)
    grad_ffn_in = jnp.sum(grad_route_in, axis=1, dtype=single_precision)
    chosen = (own_routes[:, :, None] == jnp.arange(experts, dtype=jnp.int32)[None, None, :]).astype(
        single_precision
    )
    grad_probs = jnp.sum(route_grad_weight[:, :, None] * chosen, axis=1)
    grad_logits = (
        router_probs * (grad_probs - jnp.sum(router_probs * grad_probs, axis=-1, keepdims=True))
    ).astype(bf16)
    grad_router = jnp.einsum(
        "td,te->de", ffn_in, grad_logits, preferred_element_type=single_precision
    )
    grad_ffn_in = grad_ffn_in + jnp.einsum(
        "te,de->td", grad_logits, router_weight, preferred_element_type=single_precision
    )
    grad_mid_norm, grad_ffn_gain = rms_backward(grad_ffn_in, normed2, factor2, ffn_gain)
    grad_mid = grad + grad_mid_norm
    grad_mid_b = grad_mid.astype(bf16)
    grad_att = (
        jnp.einsum("td,dq->tq", grad_mid_b, out_full, preferred_element_type=single_precision)
        .astype(bf16)
        .reshape(seq_tok, heads, head_dim)
    )
    delta = jnp.sum(
        grad_att.astype(single_precision)
        * attended.reshape(seq_tok, heads, head_dim).astype(single_precision),
        axis=-1,
    )
    probs = jnp.exp(masked_scores() - lse)
    grad_vals = jnp.einsum(
        "hqk,qhd->khd", probs.astype(bf16), grad_att, preferred_element_type=single_precision
    )
    grad_p = jnp.einsum("qhd,khd->hqk", grad_att, vals3, preferred_element_type=single_precision)
    grad_scores = (probs * (grad_p - delta.T[:, :, None])).astype(bf16)
    grad_queries = (
        jnp.einsum("hqk,khd->qhd", grad_scores, keys3, preferred_element_type=single_precision)
        * scale
    )
    grad_keys_all = (
        jnp.einsum("hqk,qhd->khd", grad_scores, queries, preferred_element_type=single_precision)
        * scale
    )
    grad_keys_values = sum_context_halves(
        jnp.stack(
            [grad_keys_all.reshape(seq_len, heads_width), grad_vals.reshape(seq_len, heads_width)],
            axis=1,
        )
    )
    grad_keys = grad_keys_values[:, 0]
    grad_values = grad_keys_values[:, 1]
    grad_qn = rotate(grad_queries, cosine, sine, -1.0).reshape(seq_tok, heads_width)
    grad_kn = rotate(grad_keys.reshape(seq_tok, heads, head_dim), cosine, sine, -1.0).reshape(
        seq_tok, heads_width
    )
    grad_q_raw, grad_q_gain = rms_backward(grad_qn, q_normed, q_factor, q_gain)
    grad_k_raw, grad_k_gain = rms_backward(grad_kn, k_normed, k_factor, k_gain)
    projected_gradient = jnp.stack(
        [grad_q_raw, grad_k_raw, grad_values, jnp.zeros_like(grad_values)], axis=1
    ).astype(bf16)
    attention_input_gradient = jnp.dot(
        projected_gradient.reshape(seq_tok, 4 * heads_width),
        weights_full.reshape(width, 4 * heads_width).T,
        preferred_element_type=single_precision,
    )
    grad_x_norm, grad_attn_gain = rms_backward(
        attention_input_gradient, normed1, factor1, attn_gain
    )
    grad_tokens = grad_mid + grad_x_norm

    def scatter_over_copies(values):
        values = lax.psum_scatter(values.astype(bf16), "dp", scatter_dimension=1, tiled=True)
        values = lax.psum_scatter(values, "context", scatter_dimension=1, tiled=True)
        return values.astype(single_precision)

    grad_in_shard = scatter_over_copies(grad_gate_up_w[0])[None]
    grad_down_shard = scatter_over_copies(grad_down[0])[None]
    left = jnp.stack([attention_input] * 3 + [grad_mid_b])
    right = jnp.concatenate([projected_gradient[:, :3].transpose(1, 0, 2), attended[None]], axis=0)
    stacked = jnp.einsum("sta,stb->sab", left, right, preferred_element_type=single_precision)
    summed = lax.psum(stacked.astype(bf16), all_axes)
    shard_rows = width // lax.axis_size(all_axes)
    start = lax.axis_index(all_axes) * shard_rows
    weight_shard = lax.dynamic_slice_in_dim(summed, start, shard_rows, axis=1).astype(
        single_precision
    )
    grad_qkv_shard = weight_shard[:3]
    grad_out_shard = weight_shard[3]
    small_sum = butterfly_sum(
        jnp.concatenate(
            [grad_attn_gain, grad_q_gain, grad_k_gain, grad_ffn_gain, grad_router.reshape(-1)]
        ),
        all_axes,
    )
    sizes = [width, heads_width, heads_width, width, width * experts]
    offsets = [sum(sizes[:n]) for n in range(len(sizes))]
    totals = [small_sum[o : o + n] for o, n in zip(offsets, sizes)]
    totals[4] = totals[4].reshape(width, experts)
    return (
        output[None],
        grad_tokens[None],
        totals[0],
        totals[1],
        totals[2],
        totals[3],
        totals[4],
        grad_qkv_shard,
        grad_out_shard,
        grad_in_shard,
        grad_down_shard,
    )


def solution(mesh):
    return jax.shard_map(
        body,
        mesh=mesh,
        in_specs=(
            P(("dp", "expert"), "context", None),
            P(("dp", "expert"), "context", None),
            P(("dp", "expert"), "context", None),
            P(("dp", "expert"), None),
            P(),
            P(),
            P(),
            P(),
            P(None, ("dp", "context", "expert"), None),
            P(("dp", "context", "expert"), None),
            P(),
            P("expert", None, None, None),
            P("expert", None, None),
        ),
        out_specs=(
            P(("dp", "expert"), "context", None),
            P(("dp", "expert"), "context", None),
            P(),
            P(),
            P(),
            P(),
            P(),
            P(None, ("dp", "context", "expert"), None),
            P(("dp", "context", "expert"), None),
            P("expert", None, ("dp", "context"), None),
            P("expert", None, ("dp", "context")),
        ),
        check_vma=False,
    )
```

profile of v0, /device:TPU:1, one launch (start us, length us, event | category | flops | bytes accessed | tf_op | source)
XLA Modules:
  0.0 1209.6 jit_solution(8714754060576962103)
XLA Ops:
  13.1 237.4 %all-gather.2.cloned.1.call-done = bf16[2048,4,2048]{2,0,1:T(8,128)(2,1)} async-done(((bf16[16,4,2048]{2,0,1:T(8,128)(2,1)}), bf16[2048,4,2048]{2,0,1:T(8,128)(2,1)}) %all-gather.2.cloned.1.call-update) | async-done | bytes 33554448 | tf_op jit(solution)/shard_map/all_gather | solution.py:137
  250.6 42.7 %copy.110 = bf16[2048,4,2048]{0,2,1:T(8,128)(2,1)} copy(bf16[2048,4,2048]{2,0,1:T(8,128)(2,1)} %all-gather.2.cloned.1.call-done) | data formatting | bytes 67108864 | tf_op jit(solution)/shard_map/all_gather | solution.py:137
  293.3 17.2 %fusion.33 = f32[3,128,2048]{2,1,0:T(8,128)S(1)} fusion(bf16[2048,4,2048]{0,2,1:T(8,128)(2,1)} %copy.110, bf16[1,128,2048]{2,1,0:T(8,128)(2,1)S(1)} %fusion.83), kind=kOutput, calls=%fused_computation.54 | convolution fusion | flops 3221225472 | bytes 37224448 | tf_op jit(solution)/shard_map/slice | solution.py:149
  317.9 21.8 %collective-permute-done = bf16[128,2,2048]{2,0,1:T(8,128)(2,1)S(1)} collective-permute-done((bf16[128,2,2048]{2,0,1:T(8,128)(2,1)}, bf16[128,2,2048]{2,0,1:T(8,128)(2,1)S(1)}, u32[]{:S(2)}, u32[]{:S(2)}) %collective-permute-start) | collective-permute-done | bytes 1048608 | tf_op jit(solution)/shard_map/ppermute | solution.py:71
  381.5 10.0 scatter_custom_fusion.1
  391.5 49.0 %all-to-all-done = bf16[32,40,2048]{2,1,0:T(8,128)(2,1)} async-done(((bf16[32,40,2048]{2,1,0:T(8,128)(2,1)}), bf16[32,40,2048]{2,1,0:T(8,128)(2,1)}, u32[]{:S(2)}, u32[]{:S(2)}) %all-to-all-start) | async-done | bytes 5242912 | tf_op jit(solution)/shard_map/all_to_all | solution.py:195
  447.4 16.8 %fusion.11 = f32[1,2,1280,1024]{3,2,1,0:T(8,128)S(1)} fusion(bf16[1280,2048,1]{1,0,2:T(8,128)(2,1)} %bitcast.24, bf16[1,2,2048,1024]{3,2,1,0:T(8,128)(2,1)} %param.24), kind=kOutput, calls=%fused_computation.25 | convolution fusion | flops 10737418240 | bytes 24117248 | tf_op jit(solution)/shard_map/lrd,lkdh->lkrh/dot_general | solution.py:203
  470.9 42.7 %all-to-all-done.2 = bf16[32,40,2048]{2,1,0:T(8,128)(2,1)} async-done(((bf16[32,40,2048]{2,1,0:T(8,128)(2,1)}), bf16[32,40,2048]{2,1,0:T(8,128)(2,1)}, u32[]{:S(2)}, u32[]{:S(2)}) %all-to-all-start.2) | async-done | bytes 5242912 | tf_op jit(solution)/shard_map/all_to_all | solution.py:223
  513.6 10.1 convolution_convert_fusion.2
  524.3 13.1 %fusion.41 = (bf16[1,1,1280,1024]{3,2,1,0:T(8,128)(2,1)S(1)}, bf16[1,1,1280,1024]{3,2,1,0:T(8,128)(2,1)S(1)}) fusion(f32[1,2,1280,1024]{3,2,1,0:T(8,128)} %copy-done.5, bf16[1280,2048]{1,0:T(8,128)(2,1)} %bitcast.41, bf16[1,1024,2048]{2,1,0:T(8,128)(2,1)} %param.25), kind=kOutput, calls=%fused_computation.60 | convolution fusion | flops 5385748480 | bytes 25165824 | tf_op jit(solution)/shard_map/lrd,lhd->lrh/dot_general | solution.py:231
  539.7 16.1 %convert_bitcast_fusion = bf16[2,2048,1024]{1,2,0:T(8,128)(2,1)} fusion(bf16[1280,2048,1]{1,0,2:T(8,128)(2,1)} %bitcast.24, bf16[1,1,1280,1024]{3,2,1,0:T(8,128)(2,1)S(1)} %get-tuple-element.74, bf16[1,1,1280,1024]{3,2,1,0:T(8,128)(2,1)S(1)} %get-tuple-element.73), kind=kOutput, calls=%fused_computation.21 | convolution fusion | flops 10744233984 | bytes 18874368 | tf_op jit(solution)/shard_map/lrd,lkrh->lkdh/dot_general | solution.py:240
  574.5 18.7 %bitcast_convert_fusion = bf16[1280,2048]{1,0:T(8,128)(2,1)} fusion(bf16[1,2,2048,1024]{3,2,1,0:T(8,128)(2,1)} %param.24, bf16[1,1,1280,1024]{3,2,1,0:T(8,128)(2,1)} %copy-done.64, bf16[1,1,1280,1024]{3,2,1,0:T(8,128)(2,1)} %copy-done.63), kind=kOutput, calls=%fused_computation.11 | convolution fusion | flops 10742661120 | bytes 18874368 | tf_op jit(solution)/shard_map/lkrh,lkdh->lrd/dot_general | solution.py:243
  593.2 46.6 %all-to-all-done.1 = bf16[32,40,2048]{2,1,0:T(8,128)(2,1)} async-done(((bf16[32,40,2048]{2,1,0:T(8,128)(2,1)}), bf16[32,40,2048]{2,1,0:T(8,128)(2,1)}, u32[]{:S(2)}, u32[]{:S(2)}) %all-to-all-start.1) | async-done | bytes 5242912 | tf_op jit(solution)/shard_map/all_to_all | solution.py:211
  639.9 11.2 all-to-all-start.3
  653.5 12.2 %gather_fusion = bf16[1024,2048]{1,0:T(8,128)(2,1)} fusion(bf16[1280,2048]{1,0:T(8,128)(2,1)} %bitcast.34, s32[1024]{0:T(1024)S(1)} %broadcast_clamp_fusion), kind=kCustom, calls=%fused_computation | custom fusion | bytes 8392704 | tf_op jit(solution)/shard_map/gather | solution.py:214
  670.7 46.8 %all-to-all-done.3 = bf16[32,40,2048]{2,1,0:T(8,128)(2,1)} async-done(((bf16[32,40,2048]{2,1,0:T(8,128)(2,1)}), bf16[32,40,2048]{2,1,0:T(8,128)(2,1)}, u32[]{:S(2)}, u32[]{:S(2)}) %all-to-all-start.3) | async-done | bytes 5242912 | tf_op jit(solution)/shard_map/all_to_all | solution.py:246
  717.5 12.0 gather_fusion.1
  767.1 13.0 %collective-permute-done.1 = bf16[128,2,2048]{2,0,1:T(8,128)(2,1)} collective-permute-done((bf16[128,2,2048]{2,0,1:T(8,128)(2,1)}, bf16[128,2,2048]{2,0,1:T(8,128)(2,1)}, u32[]{:S(2)}, u32[]{:S(2)}) %collective-permute-start.1) | collective-permute-done | bytes 1048608 | tf_op jit(solution)/shard_map/ppermute | solution.py:71
  799.6 14.3 %convolution_convert_fusion = bf16[4,2048,2048]{2,1,0:T(8,128)(2,1)} fusion(bf16[1,128,2048]{2,1,0:T(8,128)(2,1)S(1)} %copy-done.26, bf16[1,128,2048]{2,1,0:T(8,128)(2,1)S(1)} %copy-done.2, bf16[1,128,2048]{2,1,0:T(8,128)(2,1)S(1)} %copy-done.25, bf16[3,128,2048]{2,1,0:T(8,128)(2,1)S(1)} %maximum_bitcast_fusion.3), kind=kOutput, calls=%fused_computation.8 | convolution fusion | flops 4315938816 | bytes 36700160 | tf_op jit(solution)/shard_map/sta,stb->sab/dot_general | solution.py:331
  815.6 18.4 %fusion.80 = (f32[2048]{0:T(1024)S(1)}, f32[128]{0:T(128)S(1)}, f32[128,2048]{1,0:T(8,128)}) fusion(bf16[1,128,2048]{2,1,0:T(8,128)(2,1)S(1)} %copy-done.15, f32[128]{0:T(128)S(1)} %copy-done.62, f32[2048]{0:T(1024)S(1)} %copy-done.51, bf16[2048,4,2048]{2,0,1:T(8,128)(2,1)} %all-gather.2.cloned.1.call-done, bf16[128,1,2048]{2,0,1:T(8,128)(2,1)} %slice.230, ...), kind=kOutput, calls=%fused_computation.116 | convolution fusion | flops 4299945984 | bytes 36717576 | tf_op jit(solution)/shard_map/dot_general | solution.py:312
  852.0 15.6 %collective-permute-start.4 = (f32[73728]{0:T(1024)S(1)}, f32[73728]{0:T(1024)S(1)}, u32[]{:S(2)}, u32[]{:S(2)}) collective-permute-start(f32[73728]{0:T(1024)S(1)} %add.208), channel_id=1, source_target_pairs={{0,4},{1,5},{2,6},{3,7},{4,0},{5,1},{6,2},{7,3},{8,12},{9,13},{10,... | collective-permute-start | bytes 884744 | tf_op jit(solution)/shard_map/ppermute | solution.py:98
  909.0 14.1 %collective-permute-start.8 = (f32[73728]{0:T(1024)S(1)}, f32[73728]{0:T(1024)S(1)}, u32[]{:S(2)}, u32[]{:S(2)}) collective-permute-start(f32[73728]{0:T(1024)S(1)} %add.212), channel_id=1, source_target_pairs={{0,64},{1,65},{2,66},{3,67},{4,68},{5,69},{6,70},{7,71},{8,72},{9,... | collective-permute-start | bytes 884744 | tf_op jit(solution)/shard_map/ppermute | solution.py:98
  929.3 206.1 %all-reduce.2.cloned.1.call-done = bf16[4,2048,2048]{2,1,0:T(8,128)(2,1)} async-done(((bf16[4,2048,2048]{2,1,0:T(8,128)(2,1)}), bf16[4,2048,2048]{2,1,0:T(8,128)(2,1)}) %all-reduce.2.cloned.1.call-update) | async-done | bytes 33554448 | tf_op jit(solution)/shard_map/psum | solution.py:332
  1137.8 55.3 %reduce-scatter.7.cloned.1.call-done = bf16[2,512,1024]{1,2,0:T(8,128)(2,1)} async-done(((bf16[2,1024,1024]{1,2,0:T(8,128)(2,1)}), bf16[2,512,1024]{1,2,0:T(8,128)(2,1)}) %reduce-scatter.7.cloned.1.call-update) | async-done | bytes 2097168 | tf_op jit(solution)/shard_map/reduce_scatter | solution.py:324
  (279 shorter events, 232.8 us)
Async XLA Ops:
  7.2 366.5 %copy-start = (bf16[2048,32]{0,1:T(8,128)(2,1)S(1)}, bf16[2048,32]{0,1:T(8,128)(2,1)}, u32[]{:S(2)}) copy-start(bf16[2048,32]{0,1:T(8,128)(2,1)} %param.23) | copy-start | bytes 393220
  7.2 243.4 %all-gather.2.cloned.1.call-start = ((), (), s32[]{:S(2)}) async-start(), calls=%async_computation.8 | async-start | bytes 33816576 | tf_op jit(solution)/shard_map/all_gather | solution.py:137
  10.9 282.3 %copy-start.61 = (f32[128]{0:T(128)}, f32[128]{0:T(128)S(1)}, u32[]{:S(2)}) copy-start(f32[128]{0:T(128)S(1)} %add_rsqrt_fusion.3) | copy-start | bytes 1540
  11.9 301.2 %copy-start.38 = (f32[128,64]{1,0:T(8,128)}, f32[128,64]{1,0:T(8,128)S(1)}, u32[]{:S(2)}) copy-start(f32[128,64]{1,0:T(8,128)S(1)} %get-tuple-element.104) | copy-start | bytes 98308
  13.1 280.1 %copy-start.1 = (bf16[1,128,2048]{2,1,0:T(8,128)(2,1)}, bf16[1,128,2048]{2,1,0:T(8,128)(2,1)S(1)}, u32[]{:S(2)}) copy-start(bf16[1,128,2048]{2,1,0:T(8,128)(2,1)S(1)} %fusion.83) | copy-start | bytes 1572868
  315.8 23.9 %collective-permute-start = (bf16[128,2,2048]{2,0,1:T(8,128)(2,1)}, bf16[128,2,2048]{2,0,1:T(8,128)(2,1)S(1)}, u32[]{:S(2)}, u32[]{:S(2)}) collective-permute-start(bf16[128,2,2048]{2,0,1:T(8,128)(2,1)} %pad_maximum_fusion.2), channel_id=1, source_target_pairs={{0,32},{32,0},{1,33},{33,1},{2,34},{34,2},{3,35},{35,3},{4,36},{36... | collective-permute-start | bytes 3145736 | tf_op jit(solution)/shard_map/ppermute | solution.py:71
  366.3 74.2 %all-to-all-start = ((bf16[32,40,2048]{2,1,0:T(8,128)(2,1)}), bf16[32,40,2048]{2,1,0:T(8,128)(2,1)}, u32[]{:S(2)}, u32[]{:S(2)}) async-start(bf16[32,40,2048]{2,1,0:T(8,128)(2,1)} %bitcast.277), calls=%async_computation | async-start | bytes 10485760 | tf_op jit(solution)/shard_map/all_to_all | solution.py:195
  440.5 73.1 %all-to-all-start.2 = ((bf16[32,40,2048]{2,1,0:T(8,128)(2,1)}), bf16[32,40,2048]{2,1,0:T(8,128)(2,1)}, u32[]{:S(2)}, u32[]{:S(2)}) async-start(bf16[32,40,2048]{2,1,0:T(8,128)(2,1)} %bitcast.278), calls=%async_computation.2 | async-start | bytes 10485760 | tf_op jit(solution)/shard_map/all_to_all | solution.py:223
  447.1 319.9 %reduce-scatter.9.cloned.1.call-start = ((), (), s32[]{:S(2)}) async-start(), calls=%async_computation.12 | async-start | bytes 6291456 | tf_op jit(solution)/shard_map/reduce_scatter | solution.py:323
  523.8 290.3 %reduce-scatter.5.cloned.1.call-start = ((), (), s32[]{:S(2)}) async-start(), calls=%async_computation.10 | async-start | bytes 12582912 | tf_op jit(solution)/shard_map/reduce_scatter | solution.py:323
  565.7 74.2 %all-to-all-start.1 = ((bf16[32,40,2048]{2,1,0:T(8,128)(2,1)}), bf16[32,40,2048]{2,1,0:T(8,128)(2,1)}, u32[]{:S(2)}, u32[]{:S(2)}) async-start(bf16[32,40,2048]{2,1,0:T(8,128)(2,1)} %bitcast.284), calls=%async_computation.1 | async-start | bytes 10485760 | tf_op jit(solution)/shard_map/all_to_all | solution.py:211
  639.9 77.6 %all-to-all-start.3 = ((bf16[32,40,2048]{2,1,0:T(8,128)(2,1)}), bf16[32,40,2048]{2,1,0:T(8,128)(2,1)}, u32[]{:S(2)}, u32[]{:S(2)}) async-start(bf16[32,40,2048]{2,1,0:T(8,128)(2,1)} %bitcast.283), calls=%async_computation.3 | async-start | bytes 10485760 | tf_op jit(solution)/shard_map/all_to_all | solution.py:246
  651.1 275.3 %reduce-scatter.11.cloned.1.call-start = ((), (), s32[]{:S(2)}) async-start(), calls=%async_computation.13 | async-start | bytes 3145728 | tf_op jit(solution)/shard_map/reduce_scatter | solution.py:324
  761.4 18.6 %collective-permute-start.1 = (bf16[128,2,2048]{2,0,1:T(8,128)(2,1)}, bf16[128,2,2048]{2,0,1:T(8,128)(2,1)}, u32[]{:S(2)}, u32[]{:S(2)}) collective-permute-start(bf16[128,2,2048]{2,0,1:T(8,128)(2,1)} %select_convert_fusion), channel_id=1, source_target_pairs={{0,32},{32,0},{1,33},{33,1},{2,34},{34,2},{3,35},{35,3},{4,36},{36... | collective-permute-start | bytes 3145736 | tf_op jit(solution)/shard_map/ppermute | solution.py:71
  767.0 368.4 %all-reduce.2.cloned.1.call-start = ((), (), s32[]{:S(2)}) async-start(), calls=%async_computation.9 | async-start | bytes 67108864 | tf_op jit(solution)/shard_map/psum | solution.py:332
  813.9 379.2 %reduce-scatter.7.cloned.1.call-start = ((), (), s32[]{:S(2)}) async-start(), calls=%async_computation.11 | async-start | bytes 6291456 | tf_op jit(solution)/shard_map/reduce_scatter | solution.py:324
  834.0 89.1 %copy-start.37 = (f32[128,2048]{1,0:T(8,128)S(1)}, f32[128,2048]{1,0:T(8,128)}, u32[]{:S(2)}) copy-start(f32[128,2048]{1,0:T(8,128)} %get-tuple-element.110) | copy-start | bytes 3145732
  834.0 7.2 collective-permute-start.2
  841.2 10.7 collective-permute-start.3
  852.0 22.8 %collective-permute-start.4 = (f32[73728]{0:T(1024)S(1)}, f32[73728]{0:T(1024)S(1)}, u32[]{:S(2)}, u32[]{:S(2)}) collective-permute-start(f32[73728]{0:T(1024)S(1)} %add.208), channel_id=1, source_target_pairs={{0,4},{1,5},{2,6},{3,7},{4,0},{5,1},{6,2},{7,3},{8,12},{9,13},{10,... | collective-permute-start | bytes 884744 | tf_op jit(solution)/shard_map/ppermute | solution.py:98
  874.8 9.0 collective-permute-start.5
  883.9 14.0 %collective-permute-start.6 = (f32[73728]{0:T(1024)S(1)}, f32[73728]{0:T(1024)S(1)}, u32[]{:S(2)}, u32[]{:S(2)}) collective-permute-start(f32[73728]{0:T(1024)S(1)} %add.210), channel_id=1, source_target_pairs={{0,16},{1,17},{2,18},{3,19},{4,20},{5,21},{6,22},{7,23},{8,24},{9,... | collective-permute-start | bytes 884744 | tf_op jit(solution)/shard_map/ppermute | solution.py:98
  897.9 10.1 collective-permute-start.7
  909.0 15.4 %collective-permute-start.8 = (f32[73728]{0:T(1024)S(1)}, f32[73728]{0:T(1024)S(1)}, u32[]{:S(2)}, u32[]{:S(2)}) collective-permute-start(f32[73728]{0:T(1024)S(1)} %add.212), channel_id=1, source_target_pairs={{0,64},{1,65},{2,66},{3,67},{4,68},{5,69},{6,70},{7,71},{8,72},{9,... | collective-permute-start | bytes 884744 | tf_op jit(solution)/shard_map/ppermute | solution.py:98
  (60 other events, 387.7 us)
Sparse Core Ops, SparseCore 0:
  10.3 240.1 all-gather.1
  523.9 21.7 reduce-scatter.8
  556.0 26.1 reduce-scatter.4
  767.1 43.3 reduce-scatter.10
  816.8 318.5 all-reduce.1
  1137.8 55.2 reduce-scatter.6
where the time goes:
time: 1220 us; the launch traced here: 1210 us
  waiting for transfers between devices  763 us (63%)
  matrix products  165 us (14%)
  local copies, waits for them, and re-layouts  128 us (10%)
  starting transfers between devices  80.6 us (7%)
  other arithmetic  57.7 us (5%)
  between operations  15.5 us (1%)
    all_gather x1, waiting for transfers between devices, body(): lax.all_gather(jnp.concatenate([qkv_weight.transpose(1, 0, 2), out_weight...  237 us
    psum x1, waiting for transfers between devices, body(): summed = lax.psum(stacked.astype(bf16), all_axes)  206 us
    reduce_scatter x2, waiting for transfers between devices, scatter_over_copies(): lax.psum_scatter(values, 'context', scatter_dimension=1, tiled=True)  55.3 us
    all_to_all x1, waiting for transfers between devices, body(): lax.all_to_all(send.reshape(sources, local_experts * capacity, width), 'e...  49 us
    all_to_all x1, waiting for transfers between devices, body(): lax.all_to_all(source_major(grad_rows_in, sources, capacity), 'expert', s...  46.8 us
    all_to_all x1, waiting for transfers between devices, body(): lax.all_to_all(source_major(results, sources, capacity), 'expert', split_...  46.6 us
    ppermute x7, starting transfers between devices, butterfly_sum(): received = lax.ppermute(values, axes, partner)  44 us
    ppermute x7, waiting for transfers between devices, butterfly_sum(): received = lax.ppermute(values, axes, partner)  43.8 us
  transfers between devices with their start and end apart: 19, of which 15 were waited for; matrix products, arithmetic and copies ran while one was open for 19% of the time, Pallas kernels for 0%

commit v1 on v0

--- a/solution.py
+++ b/solution.py
@@ -134,11 +134,18 @@
     normed1, factor1 = rms_forward(x)
     attention_input = (normed1 * attn_gain).astype(bf16)
     all_axes = ("dp", "context", "expert")
-    weights_full = lax.all_gather(
-        jnp.concatenate([qkv_weight.transpose(1, 0, 2), out_weight[:, None, :]], axis=1),
-        all_axes,
+    weights_full = jnp.concatenate(
+        lax.all_to_all(
+            jnp.stack(
+                [jnp.concatenate([qkv_weight.transpose(1, 0, 2), out_weight[:, None, :]], axis=1)]
+                * lax.axis_size(all_axes),
+                axis=0,
+            ),
+            all_axes,
+            0,
+            0,
+        ),
         axis=0,
-        tiled=True,
     )
     out_full = weights_full[:, 3, :]
     projected_all = jnp.dot(

time: 1220 us -> 1710 us (1.40)
  waiting for transfers between devices: 763 us -> 1080 us
  local copies, waits for them, and re-layouts: 128 us -> 237 us
  starting transfers between devices: 80.6 us -> 143 us
    all_to_all x0 -> x1, waiting for transfers between devices: none -> 585 us  [body(): lax.all_to_all(jnp.stack([jnp.concatenate([qkv_weight.transpose(1, 0, 2),...]
    all_gather x1 -> x0, waiting for transfers between devices: 237 us -> none  [body(): lax.all_gather(jnp.concatenate([qkv_weight.transpose(1, 0, 2), out_weight...]
    all_to_all x0 -> x2, local copies, waits for them, and re-layouts: none -> 60.5 us  [body(): lax.all_to_all(jnp.stack([jnp.concatenate([qkv_weight.transpose(1, 0, 2),...]
    reduce_scatter x2, waiting for transfers between devices: 55.3 us -> 0.01 us  [scatter_over_copies(): lax.psum_scatter(values, 'context', scatter_dimension=1, tiled=True)]
    all_to_all x1, starting transfers between devices: 7.06 us -> 58.3 us  [body(): lax.all_to_all(send.reshape(sources, local_experts * capacity, width), 'e...]
    dot_general x0 -> x1, local copies, waits for them, and re-layouts: none -> 44.4 us  [body(): jnp.dot(attention_input, weights_full.reshape(width, 4 * heads_width), pr...]
    all_gather x1 -> x0, local copies, waits for them, and re-layouts: 42.7 us -> none  [body(): lax.all_gather(jnp.concatenate([qkv_weight.transpose(1, 0, 2), out_weight...]
    psum x1, waiting for transfers between devices: 206 us -> 244 us  [body(): summed = lax.psum(stacked.astype(bf16), all_axes)]
  transfers between devices with their start and end apart: 19 -> 19, of which waited for: 15 -> 13; matrix products, arithmetic and copies ran while one was open for 19% -> 15% of each run, Pallas kernels for 0% -> 0%
where the time goes in v1:
time: 1710 us; the launch traced here: 1700 us
  waiting for transfers between devices  1080 us (63%)
  local copies, waits for them, and re-layouts  237 us (14%)
  matrix products  163 us (10%)
  starting transfers between devices  143 us (8%)
  other arithmetic  58.5 us (3%)
    all_to_all x1, waiting for transfers between devices, body(): lax.all_to_all(jnp.stack([jnp.concatenate([qkv_weight.transpose(1, 0, 2),...  585 us
    psum x1, waiting for transfers between devices, body(): summed = lax.psum(stacked.astype(bf16), all_axes)  244 us
    all_to_all x2, local copies, waits for them, and re-layouts, body(): lax.all_to_all(jnp.stack([jnp.concatenate([qkv_weight.transpose(1, 0, 2),...  60.5 us
    all_to_all x1, starting transfers between devices, body(): lax.all_to_all(send.reshape(sources, local_experts * capacity, width), 'e...  58.3 us
    unnamed x155, local copies, waits for them, and re-layouts  53.1 us
    ppermute x7, waiting for transfers between devices, butterfly_sum(): received = lax.ppermute(values, axes, partner)  49.3 us
    all_to_all x1, waiting for transfers between devices, body(): lax.all_to_all(source_major(results, sources, capacity), 'expert', split_...  49 us
    all_to_all x1, waiting for transfers between devices, body(): lax.all_to_all(send.reshape(sources, local_experts * capacity, width), 'e...  47.9 us
  transfers between devices with their start and end apart: 19, of which 13 were waited for; matrix products, arithmetic and copies ran while one was open for 15% of the time, Pallas kernels for 0%

profile of v1, /device:TPU:1, one launch (start us, length us, event | category | flops | bytes accessed | tf_op | source)
XLA Modules:
  0.0 1700.5 jit_solution(8034296440464740312)
XLA Ops:
  20.1 12.0 all-to-all-start
  33.5 585.1 %all-to-all-done = bf16[128,16,4,2048]{3,1,2,0:T(8,128)(2,1)} async-done(((bf16[128,16,4,2048]{3,1,2,0:T(8,128)(2,1)}), bf16[128,16,4,2048]{3,1,2,0:T(8,128)(2,1)}, u32[]{:S(2)}, u32[]{:S(2)}) %all-to-all-start) | async-done | bytes 33554464 | tf_op jit(solution)/shard_map/all_to_all | solution.py:138
  618.6 37.6 %copy.149 = bf16[128,16,4,2048]{3,2,1,0:T(4,128)(2,1)} copy(bf16[128,16,4,2048]{3,1,2,0:T(8,128)(2,1)} %all-to-all-done) | data formatting | bytes 67108864 | tf_op jit(solution)/shard_map/all_to_all | solution.py:138
  656.2 30.1 %copy.197 = bf16[256,8,4,2048]{3,1,2,0:T(8,128)(2,1)} copy(bf16[256,8,4,2048]{3,2,1,0:T(4,128)(2,1)} %bitcast.279) | data formatting | bytes 67108864
  686.2 44.4 %copy.150 = bf16[8192,2048]{1,0:T(8,128)(2,1)} copy(bf16[8192,2048]{0,1:T(8,128)(2,1)} %bitcast.276) | data formatting | bytes 67108864 | tf_op jit(solution)/shard_map/dot_general | solution.py:151
  730.7 17.2 %convolution_bitcast_fusion = f32[3,128,2048]{2,1,0:T(8,128)S(1)} fusion(bf16[4,2048,2048]{2,1,0:T(8,128)(2,1)} %bitcast.278, bf16[1,128,2048]{2,1,0:T(8,128)(2,1)S(1)} %fusion.72), kind=kOutput, calls=%fused_computation.52 | convolution fusion | flops 3221225472 | bytes 37224448 | tf_op jit(solution)/shard_map/slice | solution.py:156
  753.2 16.4 collective-permute-start
  770.6 23.0 %copy.156 = bf16[128,16,4,2048]{3,1,0,2:T(8,128)(2,1)} copy(bf16[128,16,4,2048]{3,1,2,0:T(8,128)(2,1)} %all-to-all-done) | data formatting | bytes 67108864 | tf_op jit(solution)/shard_map/all_to_all | solution.py:138
  823.8 58.3 %all-to-all-start.1 = ((bf16[32,40,2048]{2,1,0:T(8,128)(2,1)}), bf16[32,40,2048]{2,1,0:T(8,128)(2,1)}, u32[]{:S(2)}, u32[]{:S(2)}) async-start(bf16[32,40,2048]{2,1,0:T(8,128)(2,1)} %bitcast.282), calls=%async_computation.1 | async-start | bytes 10485760 | tf_op jit(solution)/shard_map/all_to_all | solution.py:202
  900.4 47.9 %all-to-all-done.1 = bf16[32,40,2048]{2,1,0:T(8,128)(2,1)} async-done(((bf16[32,40,2048]{2,1,0:T(8,128)(2,1)}), bf16[32,40,2048]{2,1,0:T(8,128)(2,1)}, u32[]{:S(2)}, u32[]{:S(2)}) %all-to-all-start.1) | async-done | bytes 5242912 | tf_op jit(solution)/shard_map/all_to_all | solution.py:202
  958.4 16.8 fusion.9
  981.9 42.4 %all-to-all-done.3 = bf16[32,40,2048]{2,1,0:T(8,128)(2,1)} async-done(((bf16[32,40,2048]{2,1,0:T(8,128)(2,1)}), bf16[32,40,2048]{2,1,0:T(8,128)(2,1)}, u32[]{:S(2)}, u32[]{:S(2)}) %all-to-all-start.3) | async-done | bytes 5242912 | tf_op jit(solution)/shard_map/all_to_all | solution.py:230
  1034.7 13.1 fusion.36
  1050.6 16.0 convert_bitcast_fusion
  1086.0 17.3 %bitcast_convert_fusion = bf16[1280,2048]{1,0:T(8,128)(2,1)} fusion(bf16[1,2,2048,1024]{3,2,1,0:T(8,128)(2,1)} %param.24, bf16[1,1,1280,1024]{3,2,1,0:T(8,128)(2,1)} %copy-done.70, bf16[1,1,1280,1024]{3,2,1,0:T(8,128)(2,1)} %copy-done.69), kind=kOutput, calls=%fused_computation.9 | convolution fusion | flops 10742661120 | bytes 18874368 | tf_op jit(solution)/shard_map/lkrh,lkdh->lrd/dot_general | solution.py:250
  1103.3 49.0 %all-to-all-done.2 = bf16[32,40,2048]{2,1,0:T(8,128)(2,1)} async-done(((bf16[32,40,2048]{2,1,0:T(8,128)(2,1)}), bf16[32,40,2048]{2,1,0:T(8,128)(2,1)}, u32[]{:S(2)}, u32[]{:S(2)}) %all-to-all-start.2) | async-done | bytes 5242912 | tf_op jit(solution)/shard_map/all_to_all | solution.py:218
  1164.5 12.4 gather_fusion
  1181.9 46.2 %all-to-all-done.4 = bf16[32,40,2048]{2,1,0:T(8,128)(2,1)} async-done(((bf16[32,40,2048]{2,1,0:T(8,128)(2,1)}), bf16[32,40,2048]{2,1,0:T(8,128)(2,1)}, u32[]{:S(2)}, u32[]{:S(2)}) %all-to-all-start.4) | async-done | bytes 5242912 | tf_op jit(solution)/shard_map/all_to_all | solution.py:253
  1228.1 12.0 gather_fusion.1
  1276.6 17.9 %collective-permute-done.1 = bf16[128,2,2048]{2,0,1:T(8,128)(2,1)} collective-permute-done((bf16[128,2,2048]{2,0,1:T(8,128)(2,1)}, bf16[128,2,2048]{2,0,1:T(8,128)(2,1)}, u32[]{:S(2)}, u32[]{:S(2)}) %collective-permute-start.1) | collective-permute-done | bytes 1048608 | tf_op jit(solution)/shard_map/ppermute | solution.py:71
  1314.6 14.3 convolution_convert_fusion
  1336.2 17.9 %fusion.69 = (f32[2048]{0:T(1024)S(1)}, f32[128]{0:T(128)}, f32[128,2048]{1,0:T(8,128)}) fusion(bf16[1,128,2048]{2,1,0:T(8,128)(2,1)S(1)} %copy-done.13, f32[128]{0:T(128)S(1)} %copy-done.64, f32[2048]{0:T(1024)S(1)} %copy-done.52, bf16[128,8192]{0,1:T(8,128)(2,1)S(1)} %bitcast.284, bf16[2048,8192]{1,0:T(8,128)(2,1)} %bitcast.277), kind=kOutput, calls=%fused_computation.108 | convolution fusion | flops 4296800256 | bytes 37241856 | tf_op jit(solution)/shard_map/dot_general | solution.py:319
  1354.3 13.1 collective-permute-done.2
  1437.1 244.2 %all-reduce.2.cloned.1.call-done = bf16[4,2048,2048]{2,1,0:T(8,128)(2,1)} async-done(((bf16[4,2048,2048]{2,1,0:T(8,128)(2,1)}), bf16[4,2048,2048]{2,1,0:T(8,128)(2,1)}) %all-reduce.2.cloned.1.call-update) | async-done | bytes 33554448 | tf_op jit(solution)/shard_map/psum | solution.py:339
  (296 shorter events, 279.1 us)
Async XLA Ops:
  8.0 874.4 %copy-start = (bf16[2048,32]{0,1:T(8,128)(2,1)S(1)}, bf16[2048,32]{0,1:T(8,128)(2,1)}, u32[]{:S(2)}) copy-start(bf16[2048,32]{0,1:T(8,128)(2,1)} %param.23) | copy-start | bytes 393220
  20.1 598.5 %all-to-all-start = ((bf16[128,16,4,2048]{3,1,2,0:T(8,128)(2,1)}), bf16[128,16,4,2048]{3,1,2,0:T(8,128)(2,1)}, u32[]{:S(2)}, u32[]{:S(2)}) async-start(bf16[128,16,4,2048]{3,1,2,0:T(8,128)(2,1)} %stack.21), calls=%async_computation | async-start | bytes 67108864 | tf_op jit(solution)/shard_map/all_to_all | solution.py:138
  32.4 623.8 %copy-start.63 = (f32[128]{0:T(128)}, f32[128]{0:T(128)S(1)}, u32[]{:S(2)}) copy-start(f32[128]{0:T(128)S(1)} %add_rsqrt_fusion.3) | copy-start | bytes 1540
  33.3 717.1 %copy-start.38 = (f32[128,64]{1,0:T(8,128)}, f32[128,64]{1,0:T(8,128)S(1)}, u32[]{:S(2)}) copy-start(f32[128,64]{1,0:T(8,128)S(1)} %get-tuple-element.115) | copy-start | bytes 98308
  33.5 697.1 %copy-start.1 = (bf16[1,128,2048]{2,1,0:T(8,128)(2,1)}, bf16[1,128,2048]{2,1,0:T(8,128)(2,1)S(1)}, u32[]{:S(2)}) copy-start(bf16[1,128,2048]{2,1,0:T(8,128)(2,1)S(1)} %fusion.72) | copy-start | bytes 1572868
  753.2 40.4 %collective-permute-start = (bf16[128,2,2048]{2,0,1:T(8,128)(2,1)}, bf16[128,2,2048]{2,0,1:T(8,128)(2,1)}, u32[]{:S(2)}, u32[]{:S(2)}) collective-permute-start(bf16[128,2,2048]{2,0,1:T(8,128)(2,1)} %pad_maximum_fusion.2), channel_id=1, source_target_pairs={{0,32},{32,0},{1,33},{33,1},{2,34},{34,2},{3,35},{35,3},{4,36},{36... | collective-permute-start | bytes 3145736 | tf_op jit(solution)/shard_map/ppermute | solution.py:71
  823.8 124.6 %all-to-all-start.1 = ((bf16[32,40,2048]{2,1,0:T(8,128)(2,1)}), bf16[32,40,2048]{2,1,0:T(8,128)(2,1)}, u32[]{:S(2)}, u32[]{:S(2)}) async-start(bf16[32,40,2048]{2,1,0:T(8,128)(2,1)} %bitcast.282), calls=%async_computation.1 | async-start | bytes 10485760 | tf_op jit(solution)/shard_map/all_to_all | solution.py:202
  948.3 76.0 %all-to-all-start.3 = ((bf16[32,40,2048]{2,1,0:T(8,128)(2,1)}), bf16[32,40,2048]{2,1,0:T(8,128)(2,1)}, u32[]{:S(2)}, u32[]{:S(2)}) async-start(bf16[32,40,2048]{2,1,0:T(8,128)(2,1)} %bitcast.283), calls=%async_computation.3 | async-start | bytes 10485760 | tf_op jit(solution)/shard_map/all_to_all | solution.py:230
  957.9 318.6 %reduce-scatter.9.cloned.1.call-start = ((), (), s32[]{:S(2)}) async-start(), calls=%async_computation.12 | async-start | bytes 6291456 | tf_op jit(solution)/shard_map/reduce_scatter | solution.py:330
  1034.4 294.8 %reduce-scatter.5.cloned.1.call-start = ((), (), s32[]{:S(2)}) async-start(), calls=%async_computation.10 | async-start | bytes 12582912 | tf_op jit(solution)/shard_map/reduce_scatter | solution.py:330
  1076.5 75.8 %all-to-all-start.2 = ((bf16[32,40,2048]{2,1,0:T(8,128)(2,1)}), bf16[32,40,2048]{2,1,0:T(8,128)(2,1)}, u32[]{:S(2)}, u32[]{:S(2)}) async-start(bf16[32,40,2048]{2,1,0:T(8,128)(2,1)} %bitcast.290), calls=%async_computation.2 | async-start | bytes 10485760 | tf_op jit(solution)/shard_map/all_to_all | solution.py:218
  1152.3 75.8 %all-to-all-start.4 = ((bf16[32,40,2048]{2,1,0:T(8,128)(2,1)}), bf16[32,40,2048]{2,1,0:T(8,128)(2,1)}, u32[]{:S(2)}, u32[]{:S(2)}) async-start(bf16[32,40,2048]{2,1,0:T(8,128)(2,1)} %bitcast.289), calls=%async_computation.4 | async-start | bytes 10485760 | tf_op jit(solution)/shard_map/all_to_all | solution.py:253
  1161.9 272.2 %reduce-scatter.11.cloned.1.call-start = ((), (), s32[]{:S(2)}) async-start(), calls=%async_computation.13 | async-start | bytes 3145728 | tf_op jit(solution)/shard_map/reduce_scatter | solution.py:331
  1271.8 22.7 %collective-permute-start.1 = (bf16[128,2,2048]{2,0,1:T(8,128)(2,1)}, bf16[128,2,2048]{2,0,1:T(8,128)(2,1)}, u32[]{:S(2)}, u32[]{:S(2)}) collective-permute-start(bf16[128,2,2048]{2,0,1:T(8,128)(2,1)} %select_convert_fusion), channel_id=1, source_target_pairs={{0,32},{32,0},{1,33},{33,1},{2,34},{34,2},{3,35},{35,3},{4,36},{36... | collective-permute-start | bytes 3145736 | tf_op jit(solution)/shard_map/ppermute | solution.py:71
  1276.5 404.7 %all-reduce.2.cloned.1.call-start = ((), (), s32[]{:S(2)}) async-start(), calls=%async_computation.9 | async-start | bytes 67108864 | tf_op jit(solution)/shard_map/psum | solution.py:339
  1329.0 354.7 %reduce-scatter.7.cloned.1.call-start = ((), (), s32[]{:S(2)}) async-start(), calls=%async_computation.11 | async-start | bytes 6291456 | tf_op jit(solution)/shard_map/reduce_scatter | solution.py:331
  1354.2 76.1 %copy-start.30 = (f32[128,2048]{1,0:T(8,128)S(1)}, f32[128,2048]{1,0:T(8,128)}, u32[]{:S(2)}) copy-start(f32[128,2048]{1,0:T(8,128)} %copy-done.29) | copy-start | bytes 3145732
  1354.2 13.2 collective-permute-start.2
  1367.5 13.8 collective-permute-start.3
  1381.4 13.9 collective-permute-start.4
  1395.4 7.3 collective-permute-start.5
  1402.7 8.2 collective-permute-start.6
  1410.9 9.1 collective-permute-start.7
  1420.1 12.1 collective-permute-start.8
  (66 other events, 689.8 us)
Sparse Core Ops, SparseCore 0:
  1034.6 18.2 reduce-scatter.8
  1066.8 22.3 reduce-scatter.4
  1276.7 44.3 reduce-scatter.10
  1332.0 76.5 reduce-scatter.6
Sparse Core Ops, SparseCore 1:
  1329.1 352.2 all-reduce.1
